TPU v7x, 128 devices: a whole 4x4x4 slice. The times are simulated.
128 devices in a mesh: req: 4 (over x), exp: 32 (over y, z, core).
Axes of the slice: x: 4, y: 4, z: 4, core: 2. Of those that a mesh axis runs over, the one named last changes fastest.
Arguments:
- tokens: bfloat16 [32768, 1536], P(('req', 'exp')), may hold values from -6 to 6
- token_request_slot: int32 [128, 256], P(('req', 'exp')), may hold values from 0 to 3, never falling along the last dimension, each value on 1 to 128 neighbouring positions
- request_prompt: int32 [512], P(('req', 'exp')), may hold values from 0 to 31
- request_adapter: int32 [512], P(('req', 'exp')), may hold values from 0 to 15
- prompt_page_table: int32 [512], replicated, may hold values from 0 to 511, each once
- shared_prompt_cache: bfloat16 [512, 16, 512], P(('req', 'exp')), may hold values from -180 to 180
- routes: int32 [32768, 4], P(('req', 'exp')), may hold values from 0 to 31, all different within a row; in each aligned block of 256 rows (0 to 255, 256 to 511, ...) at most 48 rows name the same one
- attention_norm_gain: bfloat16 [1536], replicated, may hold values from 0.099609375 to 1.8984375
- query_matrix: bfloat16 [1536, 1536], replicated, may hold values from -0.15625 to 0.15625
- key_value_weight: bfloat16 [1536, 512], replicated, may hold values from -0.15625 to 0.15625
- attention_output_weight: bfloat16 [1536, 1536], replicated, may hold values from -0.15625 to 0.15625
- adapter_query_down: bfloat16 [1536, 256], replicated, may hold values from -0.15625 to 0.15625
- adapter_query_up: bfloat16 [256, 1536], replicated, may hold values from -1.5 to 1.5
- adapter_output_down: bfloat16 [1536, 256], replicated, may hold values from -0.15625 to 0.15625
- adapter_output_up: bfloat16 [256, 1536], replicated, may hold values from -1.5 to 1.5
- expert_norm_gain: bfloat16 [1536], replicated, may hold values from 0.099609375 to 1.8984375
- router: bfloat16 [1536, 32], replicated, may hold values from -0.15625 to 0.15625
- expert_gate_up: bfloat16 [32, 1536, 1536], P('exp'), may hold values from -0.15625 to 0.15625
- expert_down: bfloat16 [32, 768, 1536], P('exp'), may hold values from -0.21875 to 0.21875
Outputs:
- mixed_rows: bfloat16 [32768, 1536], P(('req', 'exp'))
Inputs may be any that keep to these rules, and one draw needn't show every extreme that they name: `token_request_slot`: along a device's row the slots never fall; each of the 4 slots holds 1 to 128 tokens and one holds exactly 128. `prompt_page_table`: the entries whose index divided by 16 (rounded down) is p are the pages of prompt p in order; every page appears once. `routes`: each token names 4 different experts. Among the tokens of one device no expert is named more than 48 times, and in every draw some device's tokens name some expert exactly 48 times.
All inputs are finite; a program needn't handle non-finite values.
Results may differ from a plain program's by a relative error of at most 0.017.
The roundings to bfloat16 on the way count: a program that leaves them out, or rounds other values in their place, can miss the bound.
Values may be sent and summed in bfloat16 or wider, within the bound.
A program may use at most 128 MiB of HBM per device.

v0:
```python
import jax
import jax.numpy as jnp
from jax import lax
from jax.sharding import PartitionSpec as P

QUERY_HEADS = 12
KEY_VALUE_HEADS = 2
HEAD_WIDTH = 128
TOPK = 4
ADAPTER_RANK = 16
PPP = 16
PROMPT_LENGTH = 256
EPSILON = 1e-06
THETA = 1000000.0
VERY_NEGATIVE = -1e30


def rms_norm(weight_matrix, gain_vector):
    values = weight_matrix.astype(jnp.float32)
    factor = lax.rsqrt(jnp.mean(values * values, axis=-1, keepdims=True) + EPSILON)
    return (values * factor * gain_vector.astype(jnp.float32)).astype(jnp.bfloat16)


def apply_rotary(values, token_positions):
    half_width = values.shape[-1] // 2
    frequency = THETA ** (-jnp.arange(half_width).astype(jnp.float32) / half_width)
    angles = token_positions.astype(jnp.float32)[:, None] * frequency[None, :]
    cosine = jnp.cos(angles)[:, None, :]
    sine_table = jnp.sin(angles)[:, None, :]
    first_half = values[..., :half_width]
    second = values[..., half_width:]
    return jnp.concatenate(
        [first_half * cosine - second * sine_table, second * cosine + first_half * sine_table],
        axis=-1,
    )


def adapter_update(weight_matrix, down_proj, up_proj, token_adapter):
    inner = jnp.dot(weight_matrix, down_proj, preferred_element_type=jnp.float32)
    owner_slot = jnp.arange(down_proj.shape[1], dtype=jnp.int32) // ADAPTER_RANK
    inner = jnp.where(owner_slot[None, :] == token_adapter[:, None], inner, 0.0).astype(
        jnp.bfloat16
    )
    return jnp.dot(inner, up_proj, preferred_element_type=jnp.float32)


def request_info(request_row, prompt_req, adapter_req):
    new_token_count = request_row.shape[0]
    request_slot_count = prompt_req.shape[0]
    matches = request_row[:, None] == jnp.arange(request_slot_count, dtype=jnp.int32)[None, :]
    token_adapter = jnp.sum(jnp.where(matches, adapter_req[None, :], 0), axis=1)
    prompt_tok = jnp.sum(jnp.where(matches, prompt_req[None, :], 0), axis=1)
    token_index = jnp.arange(new_token_count, dtype=jnp.int32)
    first_row = jnp.min(jnp.where(matches, token_index[:, None], new_token_count), axis=0)
    start_tok = jnp.sum(jnp.where(matches, first_row[None, :], 0), axis=1)
    token_positions = PROMPT_LENGTH + token_index - start_tok
    return (token_adapter, prompt_tok, token_positions)


def apply_projection(
    tokens,
    token_adapter,
    token_positions,
    attention_norm_gain,
    query_matrix,
    key_value_weight,
    adapter_query_down,
    adapter_query_up,
):
    new_token_count = tokens.shape[0]
    normalized = rms_norm(tokens, attention_norm_gain)
    query_rows = jnp.dot(normalized, query_matrix, preferred_element_type=jnp.float32)
    query_rows = query_rows + adapter_update(
        normalized, adapter_query_down, adapter_query_up, token_adapter
    )
    query_rows = apply_rotary(
        query_rows.reshape(new_token_count, QUERY_HEADS, HEAD_WIDTH), token_positions
    ).astype(jnp.bfloat16)
    key_value_rows = jnp.dot(
        normalized, key_value_weight, preferred_element_type=jnp.float32
    ).reshape(new_token_count, 2 * KEY_VALUE_HEADS, HEAD_WIDTH)
    key_matrix = apply_rotary(key_value_rows[:, :KEY_VALUE_HEADS], token_positions).astype(
        jnp.bfloat16
    )
    value_matrix = key_value_rows[:, KEY_VALUE_HEADS:].astype(jnp.bfloat16)
    return (query_rows, key_matrix, value_matrix)


def finalize(
    attention_output,
    tokens,
    token_adapter,
    attention_output_weight,
    adapter_output_down,
    adapter_output_up,
):
    expert_mixture = jnp.dot(
        attention_output, attention_output_weight, preferred_element_type=jnp.float32
    )
    expert_mixture = expert_mixture + adapter_update(
        attention_output, adapter_output_down, adapter_output_up, token_adapter
    )
    return (tokens.astype(jnp.float32) + expert_mixture).astype(jnp.bfloat16)


def gate_weights(ffn_normed, router, routes):
    logits = jnp.dot(ffn_normed, router, preferred_element_type=jnp.float32)
    picked = jnp.take_along_axis(logits, routes, axis=1)
    squashed = jax.nn.sigmoid(picked)
    return squashed / jnp.sum(squashed, axis=1, keepdims=True)


def slot_of(routes, experts, capacity):
    flat_routes = routes.reshape(-1)
    onehot = (flat_routes[:, None] == jnp.arange(experts, dtype=jnp.int32)[None, :]).astype(
        jnp.int32
    )
    before = jnp.cumsum(onehot, axis=0) - onehot
    rank_pick = jnp.sum(before * onehot, axis=1)
    return flat_routes * capacity + rank_pick


def block_attention(running, grouped_queries, key_matrix, value_matrix, allowed):
    running_max, totals, accum = running
    scale = grouped_queries.shape[-1] ** (-0.5)
    scores = (
        jnp.einsum(
            "tkgd,nkd->tkgn", grouped_queries, key_matrix, preferred_element_type=jnp.float32
        )
        * scale
    )
    scores = jnp.where(allowed[:, None, None, :], scores, VERY_NEGATIVE)
    new_max = jnp.maximum(running_max, jnp.max(scores, axis=-1))
    factor = jnp.exp(running_max - new_max)
    weights = jnp.exp(scores - new_max[..., None])
    totals = totals * factor + jnp.sum(weights, axis=-1)
    summed = jnp.einsum(
        "tkgn,nkd->tkgd",
        weights.astype(jnp.bfloat16),
        value_matrix,
        preferred_element_type=jnp.float32,
    )
    accum = accum * factor[..., None] + summed
    return (new_max, totals, accum)


def on_device(
    tokens,
    token_request_slot,
    request_prompt,
    request_adapter,
    prompt_page_table,
    shared_prompt_cache,
    routes,
    attention_norm_gain,
    query_matrix,
    key_value_weight,
    attention_output_weight,
    adapter_query_down,
    adapter_query_up,
    adapter_output_down,
    adapter_output_up,
    expert_norm_gain,
    router,
    expert_gate_up,
    expert_down,
):
    new_token_count = tokens.shape[0]
    request_row = token_request_slot[0]
    request_slot_count = request_prompt.shape[0]
    token_adapter, prompt_tok, token_positions = request_info(
        request_row, request_prompt, request_adapter
    )
    query_rows, key_matrix, value_matrix = apply_projection(
        tokens,
        token_adapter,
        token_positions,
        attention_norm_gain,
        query_matrix,
        key_value_weight,
        adapter_query_down,
        adapter_query_up,
    )
    query_group_width = QUERY_HEADS // KEY_VALUE_HEADS
    grouped_queries = query_rows.reshape(
        new_token_count, KEY_VALUE_HEADS, query_group_width, HEAD_WIDTH
    )
    token_index = jnp.arange(new_token_count, dtype=jnp.int32)
    local_ok = (request_row[:, None] == request_row[None, :]) & (
        token_index[None, :] <= token_index[:, None]
    )
    initial = (
        jnp.full((new_token_count, KEY_VALUE_HEADS, query_group_width), VERY_NEGATIVE, jnp.float32),
        jnp.zeros((new_token_count, KEY_VALUE_HEADS, query_group_width), jnp.float32),
        jnp.zeros((new_token_count, KEY_VALUE_HEADS, query_group_width, HEAD_WIDTH), jnp.float32),
    )
    running_progress = block_attention(initial, grouped_queries, key_matrix, value_matrix, local_ok)
    requested_pages = jnp.take(prompt_page_table.reshape(-1, PPP), request_prompt, axis=0).reshape(
        -1
    )
    complete_cache = lax.all_gather(shared_prompt_cache, ("req", "exp"), axis=0, tiled=True)
    page_token_rows = jnp.take(complete_cache, requested_pages, axis=0).reshape(
        request_slot_count * PROMPT_LENGTH, 2 * KEY_VALUE_HEADS, HEAD_WIDTH
    )
    owner_slot = jnp.arange(request_slot_count * PROMPT_LENGTH, dtype=jnp.int32) // PROMPT_LENGTH
    prompt_valid_mask = request_row[:, None] == owner_slot[None, :]
    running_progress = block_attention(
        running_progress,
        grouped_queries,
        page_token_rows[:, :KEY_VALUE_HEADS],
        page_token_rows[:, KEY_VALUE_HEADS:],
        prompt_valid_mask,
    )
    running_max, totals, accum = running_progress
    attention_output = (
        (accum / totals[..., None])
        .reshape(new_token_count, QUERY_HEADS * HEAD_WIDTH)
        .astype(jnp.bfloat16)
    )
    hidden_state = finalize(
        attention_output,
        tokens,
        token_adapter,
        attention_output_weight,
        adapter_output_down,
        adapter_output_up,
    )
    ffn_normed = rms_norm(hidden_state, expert_norm_gain)
    gates = gate_weights(ffn_normed, router, routes)
    local_experts = expert_gate_up.shape[0]
    experts = local_experts * lax.axis_size("exp")
    capacity = 3 * new_token_count * TOPK // (2 * experts)
    destination = slot_of(routes, experts, capacity)
    slot_total = experts * capacity
    matches = jnp.arange(slot_total, dtype=jnp.int32)[:, None] == destination[None, :]
    source = jnp.arange(new_token_count * TOPK, dtype=jnp.int32) // TOPK
    source_tok = jnp.sum(jnp.where(matches, source[None, :], 0), axis=1)
    filled = jnp.any(matches, axis=1)
    outgoing = jnp.where(
        filled[:, None], jnp.take(ffn_normed, source_tok, axis=0), jnp.zeros((), jnp.bfloat16)
    )
    outgoing = outgoing.reshape(experts, capacity, -1)
    arrived = lax.all_to_all(outgoing, "exp", split_axis=0, concat_axis=0, tiled=True)
    sources = arrived.shape[0] // local_experts
    item_count = arrived.shape[1]
    arranged = arrived.reshape(sources, local_experts, item_count, -1)
    inner = jnp.einsum(
        "sxcd,xdf->sxcf", arranged, expert_gate_up, preferred_element_type=jnp.float32
    )
    half_width = inner.shape[-1] // 2
    units = (jax.nn.relu(inner[..., :half_width]) * inner[..., half_width:]).astype(jnp.bfloat16)
    result = jnp.einsum(
        "sxcf,xfd->sxcd", units, expert_down, preferred_element_type=jnp.float32
    ).astype(jnp.bfloat16)
    result = result.reshape(sources * local_experts, item_count, -1)
    returned = lax.all_to_all(result, "exp", split_axis=0, concat_axis=0, tiled=True)
    picked = jnp.take(returned.reshape(slot_total, -1), destination, axis=0).astype(jnp.float32)
    picked = picked.reshape(new_token_count, TOPK, -1)
    mixed_rows = hidden_state.astype(jnp.float32) + jnp.sum(gates[..., None] * picked, axis=1)
    return mixed_rows.astype(jnp.bfloat16)


def solution(mesh):
    return jax.shard_map(
        on_device,
        mesh=mesh,
        in_specs=(
            P(("req", "exp"), None),
            P(("req", "exp"), None),
            P(("req", "exp")),
            P(("req", "exp")),
            P(),
            P(("req", "exp"), None, None),
            P(("req", "exp"), None),
            P(),
            P(),
            P(),
            P(),
            P(),
            P(),
            P(),
            P(),
            P(),
            P(),
            P("exp", None, None),
            P("exp", None, None),
        ),
        out_specs=P(("req", "exp"), None),
        check_vma=False,
    )
```

profile of v0, /device:TPU:32, one launch (start us, length us, event | category | flops | bytes accessed | tf_op | source)
XLA Modules:
  0.0 310.3 jit_solution(16378191095570078321)
XLA Ops:
  14.4 9.0 %reduce-window.6 = s32[32,8,128]{2,1,0:T(8,128)S(1)} reduce-window(s32[32,8,128]{2,1,0:T(8,128)S(1)} %fusion.53, s32[]{:T(128)} %constant.133.clone.1), window={size=1x1x128 pad=0_0x0_0x127_0}, to_apply=%region_10.11 | reduce-window | flops 4161536 | bytes 262148 | tf_op jit(solution)/shard_map/reduce-window
  31.6 2.8 fusion.75
  38.4 4.9 %fusion.73 = f32[256,1536]{1,0:T(8,128)} fusion(bf16[1536,1536]{1,0:T(8,128)(2,1)} %param.27, bf16[256,1536]{1,0:T(8,128)(2,1)S(1)} %copy-done.4, f32[1536]{0:T(1024)S(1)} %convert_element_type.85, f32[256]{0:T(256)S(1)} %add_rsqrt_fusion.1), kind=kOutput, calls=%fused_computation.157 | convolution fusion | flops 1209532416 | bytes 7085056 | tf_op jit(solution)/shard_map/dot_general | solution.py:72
  43.3 4.1 %convolution_add_fusion.1 = f32[256,1536]{1,0:T(8,128)} fusion(f32[256,1536]{1,0:T(8,128)} %fusion.73, bf16[256,1536]{1,0:T(8,128)(2,1)} %param.31, bf16[1536,256]{1,0:T(8,128)(2,1)} %param.30, s32[256]{0:T(256)S(1)} %and_select_fusion, s32[256]{0:T(256)S(1)} %get-tuple-element.5, bf16[256,1536]{1,0:T(8,128)(2,1)S(1)} %copy-done.4, ...), kind=kOutput, calls=%fused_computation.27 | convolution fusion | flops 404815872 | bytes 5514240 | tf_op jit(solution)/shard_map/dot_general | solution.py:44
  47.5 3.2 %copy.100 = f32[256,1536]{0,1:T(8,128)} copy(f32[256,1536]{1,0:T(8,128)} %convolution_add_fusion.1) | data formatting | bytes 3145728 | tf_op jit(solution)/shard_map/add | solution.py:73
  61.2 3.9 %fusion.14 = (f32[256,2,6]{0,2,1:T(8,128)S(1)}, f32[2,256,256,6]{2,1,3,0:T(8,128)}) fusion(pred[256,256]{0,1:T(8,128)(4,1)S(1)} %fusion.38, bf16[256,2,6,64]{3,0,2,1:T(8,128)(2,1)} %bitcast.121, bf16[256,2,6,64]{3,0,2,1:T(8,128)(2,1)S(1)} %bitcast.119, bf16[256,2,64]{2,0,1:T(8,128)(2,1)S(1)} %get-tuple-element.14, bf16[256,2,64]{2,0,1:T(8,128)(2,1)S(1)} %get-tuple-element.13), kind=kOutput, calls=%fused_computation.32 | convolution fusion | flops 205517824 | bytes 4141056 | tf_op jit(solution)/shard_map/tkgd,nkd->tkgn/dot_general | solution.py:127
  65.1 15.9 %all-gather.2.cloned.1.call-done = bf16[512,16,512]{2,1,0:T(8,128)(2,1)} async-done(((bf16[4,16,512]{2,1,0:T(8,128)(2,1)}), bf16[512,16,512]{2,1,0:T(8,128)(2,1)}) %all-gather.2.cloned.1.call-update) | async-done | bytes 8388624 | tf_op jit(solution)/shard_map/all_gather | solution.py:201
  81.1 5.0 %gather_fusion.1 = bf16[64,16,512]{2,1,0:T(8,128)(2,1)} fusion(bf16[512,16,512]{2,1,0:T(8,128)(2,1)} %all-gather.2.cloned.1.call-done, s32[1024]{0:T(1024)S(1)} %pad_clamp_fusion.1), kind=kCustom, calls=%fused_computation.1 | custom fusion | bytes 2097408 | tf_op jit(solution)/shard_map/jit(_take)/gather | solution.py:202
  89.7 3.8 %fusion.2 = (f32[256,2,6]{0,2,1:T(8,128)S(1)}, f32[2,1024,256,6]{2,1,3,0:T(8,128)S(1)}) fusion(pred[256,1024]{0,1:T(8,128)(4,1)S(1)} %broadcast_compare_fusion, bf16[256,2,6,64]{3,0,2,1:T(8,128)(2,1)} %bitcast.122, bf16[256,2,6,64]{3,0,2,1:T(8,128)(2,1)S(1)} %bitcast.120, bf16[1024,4,128]{2,0,1:T(8,128)(2,1)S(1)} %copy_select_fusion), kind=kOutput, calls=%fused_computation.9 | convolution fusion | flops 816313344 | bytes 14561280 | tf_op jit(solution)/shard_map/tkgd,nkd->tkgn/dot_general | solution.py:127
  96.4 2.5 fusion
  99.0 4.4 %fusion.25 = bf16[256,2,6,128]{0,3,2,1:T(8,128)(2,1)S(1)} fusion(f32[2,128,256,6]{2,1,3,0:T(8,128)} %fusion.22, f32[2,1024,256,6]{2,1,3,0:T(8,128)S(1)} %get-tuple-element.25, f32[256,2,6]{0,2,1:T(8,128)S(1)} %get-tuple-element.18, pred[256,1024]{0,1:T(8,128)(4,1)S(1)} %broadcast_compare_fusion, f32[256,2,6]{0,2,1:T(8,128)S(1)} %get-tuple-element.9, ...), kind=kOutput, calls=%fused_computation.44 | convolution fusion | flops 819855360 | bytes 15794176 | tf_op jit(solution)/shard_map/tkgn,nkd->tkgd/dot_general | solution.py:137
  104.3 5.0 %fusion.78 = f32[256,1536]{1,0:T(8,128)} fusion(bf16[256,1536]{0,1:T(8,128)(2,1)S(1)} %bitcast.124, bf16[1536,1536]{1,0:T(8,128)(2,1)} %param.29), kind=kOutput, calls=%fused_computation.160 | convolution fusion | flops 1207959552 | bytes 7077888 | tf_op jit(solution)/shard_map/dot_general | solution.py:97
  109.3 4.3 %multiply_reduce_fusion.1 = (f32[256]{0:T(256)S(1)}, f32[256,1536]{1,0:T(8,128)}) fusion(f32[256,1536]{1,0:T(8,128)} %fusion.78, bf16[256,1536]{1,0:T(8,128)(2,1)} %param.33, bf16[256,1536]{0,1:T(8,128)(2,1)} %bitcast.125, bf16[1536,256]{1,0:T(8,128)(2,1)} %param.32, s32[256]{0:T(256)S(1)} %copy-done.23, s32[256]{0:T(256)S(1)} %copy-done.20, ...), kind=kOutput, calls=%fused_computation.49 | convolution fusion | flops 405602048 | bytes 6294528 | tf_op jit(solution)/shard_map/dot_general | solution.py:44
  115.3 6.2 %gather_fusion.2 = bf16[1536,1536]{1,0:T(8,128)(2,1)} fusion(bf16[256,1536]{1,0:T(8,128)(2,1)S(1)} %multiply_convert_fusion, s32[2048]{0:T(1024)S(1)} %pad_clamp_fusion), kind=kCustom, calls=%fused_computation.2 | custom fusion | bytes 9443328 | tf_op jit(solution)/shard_map/jit(_take)/gather | solution.py:240
  121.5 2.8 select_select_fusion
  124.2 61.3 %all_to_all.10 = bf16[32,48,1536]{2,1,0:T(8,128)(2,1)S(1)} all-to-all(bf16[32,48,1536]{2,1,0:T(8,128)(2,1)S(1)} %select_select_fusion), channel_id=1, replica_groups=mesh['req'=4,'exp'=32] {'exp'}, dimensions={0} | all-to-all | bytes 9437184 | tf_op jit(solution)/shard_map/all_to_all | solution.py:243
  185.6 9.7 %convolution_bitcast_fusion = f32[32,1,48,1536]{3,2,0,1:T(8,128)S(1)} fusion(bf16[32,48,1536]{2,1,0:T(8,128)(2,1)S(1)} %all_to_all.10, bf16[1,1536,1536]{2,1,0:T(8,128)(2,1)} %param.36), kind=kOutput, calls=%fused_computation.16 | convolution fusion | flops 7247757312 | bytes 18874368 | tf_op jit(solution)/shard_map/sxcd,xdf->sxcf/dot_general | solution.py:247
  195.3 5.5 %convolution_convert_fusion = bf16[32,48,1536]{2,1,0:T(8,128)(2,1)} fusion(f32[32,1,48,1536]{3,2,0,1:T(8,128)S(1)} %convolution_bitcast_fusion, bf16[1,768,1536]{2,1,0:T(8,128)(2,1)S(1)} %copy-done), kind=kOutput, calls=%fused_computation.22 | convolution fusion | flops 3629776896 | bytes 16515072 | tf_op jit(solution)/shard_map/sxcf,xfd->sxcd/dot_general | solution.py:252
  200.8 5.9 %all-to-all-start.1 = ((bf16[32,48,1536]{2,1,0:T(8,128)(2,1)}), bf16[32,48,1536]{2,1,0:T(8,128)(2,1)}, u32[]{:S(2)}, u32[]{:S(2)}) async-start(bf16[32,48,1536]{2,1,0:T(8,128)(2,1)} %convolution_convert_fusion), calls=%async_computation.1 | async-start | bytes 9437184 | tf_op jit(solution)/shard_map/all_to_all | solution.py:256
  208.0 8.7 %gather_fusion.4 = f32[1024]{0:T(1024)S(1)} fusion(f32[256,32]{0,1:T(8,128)S(1)} %fusion.79, s32[1024]{0:T(1024)S(1)} %reshape.466), kind=kCustom, calls=%fused_computation.4 | custom fusion | bytes 16384 | tf_op jit(solution)/shard_map/jit(take_along_axis)/gather | solution.py:108
  217.1 52.7 %all-to-all-done.1 = bf16[32,48,1536]{2,1,0:T(8,128)(2,1)} async-done(((bf16[32,48,1536]{2,1,0:T(8,128)(2,1)}), bf16[32,48,1536]{2,1,0:T(8,128)(2,1)}, u32[]{:S(2)}, u32[]{:S(2)}) %all-to-all-start.1) | async-done | bytes 4718624 | tf_op jit(solution)/shard_map/all_to_all | solution.py:256
  269.8 10.2 %gather_fusion.3 = bf16[1024,1536]{1,0:T(8,128)(2,1)} fusion(bf16[1536,1536]{1,0:T(8,128)(2,1)} %bitcast.31, s32[1024]{0:T(1024)S(1)} %broadcast_clamp_fusion), kind=kCustom, calls=%fused_computation.3 | custom fusion | bytes 6295552 | tf_op jit(solution)/shard_map/jit(_take)/gather | solution.py:257
  280.0 6.1 %gather.33 = bf16[256,4,1536]{2,1,0:T(4,128)(2,1)} reshape(bf16[1024,1536]{1,0:T(8,128)(2,1)} %gather_fusion.3) | data formatting | bytes 6291456 | tf_op jit(solution)/shard_map/jit(_take)/gather | solution.py:257
  286.2 16.2 %multiply_reduce_fusion = f32[256,1536]{1,0:T(8,128)S(1)} fusion(bf16[256,4,1536]{2,1,0:T(4,128)(2,1)} %gather.33, f32[256,4]{1,0:T(8,128)S(1)} %copy.110, pred[256,4]{1,0:T(8,128)(4,1)S(1)} %copy.116), kind=kLoop, calls=%fused_computation.10 | loop fusion | flops 5898240 | bytes 4723712 | tf_op jit(solution)/shard_map/reduce_sum | solution.py:259
  (132 shorter events, 42.2 us)
Async XLA Ops:
  6.5 188.8 %copy-start = (bf16[1,768,1536]{2,1,0:T(8,128)(2,1)S(1)}, bf16[1,768,1536]{2,1,0:T(8,128)(2,1)}, u32[]{:S(2)}) copy-start(bf16[1,768,1536]{2,1,0:T(8,128)(2,1)} %param.37) | copy-start | bytes 7077892
  6.5 25.1 %copy-start.4 = (bf16[256,1536]{1,0:T(8,128)(2,1)S(1)}, bf16[256,1536]{1,0:T(8,128)(2,1)}, u32[]{:S(2)}) copy-start(bf16[256,1536]{1,0:T(8,128)(2,1)} %param.19) | copy-start | bytes 2359300
  6.5 74.5 %all-gather.2.cloned.1.call-start = ((), (), s32[]{:S(2)}) async-start(), calls=%async_computation.2 | async-start | bytes 8454144 | tf_op jit(solution)/shard_map/all_gather | solution.py:201
  26.7 11.7 %copy-start.17 = (s32[1536]{0:T(1024)}, s32[1536]{0:T(1024)S(1)}, u32[]{:S(2)}) copy-start(s32[1536]{0:T(1024)S(1)} %select_reduce_fusion) | copy-start | bytes 18436
  28.4 14.9 %copy-start.19 = (s32[256]{0:T(256)}, s32[256]{0:T(256)S(1)}, u32[]{:S(2)}) copy-start(s32[256]{0:T(256)S(1)} %get-tuple-element.5) | copy-start | bytes 3076
  28.7 14.6 %copy-start.7 = (f32[256,64]{0,1:T(8,128)}, f32[256,64]{0,1:T(8,128)S(1)}, u32[]{:S(2)}) copy-start(f32[256,64]{0,1:T(8,128)S(1)} %get-tuple-element.20) | copy-start | bytes 196612
  28.8 14.6 %copy-start.9 = (f32[256,64]{0,1:T(8,128)}, f32[256,64]{0,1:T(8,128)S(1)}, u32[]{:S(2)}) copy-start(f32[256,64]{0,1:T(8,128)S(1)} %get-tuple-element.21) | copy-start | bytes 196612
  38.4 4.9 %copy-start.22 = (s32[256]{0:T(256)}, s32[256]{0:T(256)S(1)}, u32[]{:S(2)}) copy-start(s32[256]{0:T(256)S(1)} %and_select_fusion) | copy-start | bytes 3076
  47.4 3.2 %copy-start.8 = (f32[256,64]{0,1:T(8,128)S(1)}, f32[256,64]{0,1:T(8,128)}, u32[]{:S(2)}) copy-start(f32[256,64]{0,1:T(8,128)} %copy-done.7) | copy-start | bytes 196612
  47.4 3.2 %copy-start.10 = (f32[256,64]{0,1:T(8,128)S(1)}, f32[256,64]{0,1:T(8,128)}, u32[]{:S(2)}) copy-start(f32[256,64]{0,1:T(8,128)} %copy-done.9) | copy-start | bytes 196612
  65.1 23.1 %copy-start.21 = (pred[1024]{0:T(1024)(128)(4,1)S(1)}, pred[1024]{0:T(1024)(128)(4,1)}, u32[]{:S(2)}) copy-start(pred[1024]{0:T(1024)(128)(4,1)} %broadcast_in_dim.194) | copy-start | bytes 3076
  89.6 3.9 %copy-start.2 = (f32[2,256,256,6]{2,1,3,0:T(8,128)S(1)}, f32[2,256,256,6]{2,1,3,0:T(8,128)}, u32[]{:S(2)}) copy-start(f32[2,256,256,6]{2,1,3,0:T(8,128)} %get-tuple-element.23) | copy-start | bytes 9437188
  93.5 0.9 copy-start.11
  104.3 5.0 %copy-start.5 = (bf16[256,1536]{1,0:T(8,128)(2,1)S(1)}, bf16[256,1536]{1,0:T(8,128)(2,1)}, u32[]{:S(2)}) copy-start(bf16[256,1536]{1,0:T(8,128)(2,1)} %param.19) | copy-start | bytes 2359300
  104.3 5.0 %copy-start.20 = (s32[256]{0:T(256)S(1)}, s32[256]{0:T(256)}, u32[]{:S(2)}) copy-start(s32[256]{0:T(256)} %copy-done.19) | copy-start | bytes 3076
  104.3 5.0 %copy-start.23 = (s32[256]{0:T(256)S(1)}, s32[256]{0:T(256)}, u32[]{:S(2)}) copy-start(s32[256]{0:T(256)} %copy-done.22) | copy-start | bytes 3076
  109.3 4.4 %copy-start.16 = (f32[1536]{0:T(1024)S(1)}, f32[1536]{0:T(1024)}, u32[]{:S(2)}) copy-start(f32[1536]{0:T(1024)} %convert_element_type.97) | copy-start | bytes 18436
  115.3 6.2 %copy-start.18 = (pred[32,48]{1,0:T(8,128)(4,1)S(1)}, pred[32,48]{1,0:T(8,128)(4,1)}, u32[]{:S(2)}) copy-start(pred[32,48]{1,0:T(8,128)(4,1)} %broadcast_in_dim.200) | copy-start | bytes 4612
  200.8 5.9 %copy-start.15 = (s32[1024]{0:T(1024)S(1)}, s32[1024]{0:T(1024)}, u32[]{:S(2)}) copy-start(s32[1024]{0:T(1024)} %copy-done.14) | copy-start | bytes 12292
  200.8 6.0 %copy-start.12 = (s32[256,4]{0,1:T(4,128)S(1)}, s32[256,4]{0,1:T(4,128)}, u32[]{:S(2)}) copy-start(s32[256,4]{0,1:T(4,128)} %param.25) | copy-start | bytes 12292
  200.8 6.9 %copy-start.13 = (bf16[1536,32]{0,1:T(8,128)(2,1)S(1)}, bf16[1536,32]{0,1:T(8,128)(2,1)}, u32[]{:S(2)}) copy-start(bf16[1536,32]{0,1:T(8,128)(2,1)} %param.35) | copy-start | bytes 294916
  200.8 69.0 %all-to-all-start.1 = ((bf16[32,48,1536]{2,1,0:T(8,128)(2,1)}), bf16[32,48,1536]{2,1,0:T(8,128)(2,1)}, u32[]{:S(2)}, u32[]{:S(2)}) async-start(bf16[32,48,1536]{2,1,0:T(8,128)(2,1)} %convolution_convert_fusion), calls=%async_computation.1 | async-start | bytes 9437184 | tf_op jit(solution)/shard_map/all_to_all | solution.py:256
  286.2 16.3 %copy-start.3 = (f32[256,1536]{1,0:T(8,128)S(1)}, f32[256,1536]{1,0:T(8,128)}, u32[]{:S(2)}) copy-start(f32[256,1536]{1,0:T(8,128)} %get-tuple-element.27) | copy-start | bytes 4718596
  286.2 17.3 %copy-start.1 = (bf16[1,768,1536]{2,1,0:T(8,128)(2,1)S(1)}, bf16[1,768,1536]{2,1,0:T(8,128)(2,1)}, u32[]{:S(2)}) copy-start(bf16[1,768,1536]{2,1,0:T(8,128)(2,1)} %param.37) | copy-start | bytes 7077892
  (2 other events, 1.5 us)
Sparse Core Ops, SparseCore 0:
  10.3 70.6 all-gather.1
where the time goes:
time: 312 us; the launch traced here: 310 us
  waiting for transfers between devices  69.4 us (22%)
  blocking collectives  61.3 us (20%)
  local copies, waits for them, and re-layouts  58.8 us (19%)
  matrix products  50.8 us (16%)
  other arithmetic  50.3 us (16%)
  between operations  13.9 us (4%)
  starting transfers between devices  5.86 us (2%)
    all_to_all x1, blocking collectives, on_device(): lax.all_to_all(outgoing, 'exp', split_axis=0, concat_axis=0, tiled=True)  61.3 us
    all_to_all x1, waiting for transfers between devices, on_device(): lax.all_to_all(result, 'exp', split_axis=0, concat_axis=0, tiled=True)  52.7 us
    gather x2, local copies, waits for them, and re-layouts, on_device(): jnp.take(returned.reshape(slot_total, -1), destination, axis=0)  16.3 us
    reduce_sum x1, other arithmetic, on_device(): jnp.sum(gates[..., None] * picked, axis=1)  16.2 us
    all_gather x1, waiting for transfers between devices, on_device(): lax.all_gather(shared_prompt_cache, ('req', 'exp'), axis=0, tiled=True)  15.9 us
    another operation x5, other arithmetic  12.5 us
    dot_general x1, matrix products, on_device(): jnp.einsum('sxcd,xdf->sxcf', arranged, expert_gate_up, preferred_element_...  9.72 us
    gather x5, local copies, waits for them, and re-layouts, gate_weights(): picked = jnp.take_along_axis(logits, routes, axis=1)  9.13 us
  transfers between devices with their start and end apart: 2, of which 2 were waited for; matrix products, arithmetic and copies ran while one was open for 22% of the time, Pallas kernels for 0%

commit v1 on v0

--- a/solution.py
+++ b/solution.py
@@ -198,7 +198,12 @@
     requested_pages = jnp.take(prompt_page_table.reshape(-1, PPP), request_prompt, axis=0).reshape(
         -1
     )
-    complete_cache = lax.all_gather(shared_prompt_cache, ("req", "exp"), axis=0, tiled=True)
+    complete_cache = jnp.concatenate(
+        lax.all_to_all(
+            jnp.stack([shared_prompt_cache] * lax.axis_size(("req", "exp"))), ("req", "exp"), 0, 0
+        ),
+        axis=0,
+    )
     page_token_rows = jnp.take(complete_cache, requested_pages, axis=0).reshape(
         request_slot_count * PROMPT_LENGTH, 2 * KEY_VALUE_HEADS, HEAD_WIDTH
     )

time: 312 us -> 344 us (1.10)
  waiting for transfers between devices: 69.4 us -> 105 us
  between operations: 13.9 us -> 0.6 us
  starting transfers between devices: 5.86 us -> 16.5 us
  local copies, waits for them, and re-layouts: 58.8 us -> 62.8 us
  other arithmetic: 50.3 us -> 46.4 us
    all_to_all x0 -> x1, waiting for transfers between devices: none -> 51.8 us  [on_device(): lax.all_to_all(jnp.stack([shared_prompt_cache] * lax.axis_size(('req', 'e...]
    all_gather x1 -> x0, waiting for transfers between devices: 15.9 us -> none  [on_device(): lax.all_gather(shared_prompt_cache, ('req', 'exp'), axis=0, tiled=True)]
    all_to_all x0 -> x1, starting transfers between devices: none -> 10.7 us  [on_device(): lax.all_to_all(jnp.stack([shared_prompt_cache] * lax.axis_size(('req', 'e...]
    another operation x4 -> x5, local copies, waits for them, and re-layouts: 2.61 us -> 7.88 us  [the longest x1 5.27 us: on_device(): jnp.stack([shared_prompt_cache] * lax.axis_size(('req', 'exp')))]
  transfers between devices with their start and end apart: 2 -> 2, of which waited for: 2 -> 2; matrix products, arithmetic and copies ran while one was open for 22% -> 18% of each run, Pallas kernels for 0% -> 0%
where the time goes in v1:
time: 344 us; the launch traced here: 343 us
  waiting for transfers between devices  105 us (31%)
  local copies, waits for them, and re-layouts  62.8 us (18%)
  blocking collectives  61.6 us (18%)
  matrix products  50.7 us (15%)
  other arithmetic  46.4 us (13%)
  starting transfers between devices  16.5 us (5%)
    all_to_all x1, blocking collectives, on_device(): lax.all_to_all(outgoing, 'exp', split_axis=0, concat_axis=0, tiled=True)  61.6 us
    all_to_all x1, waiting for transfers between devices, on_device(): lax.all_to_all(result, 'exp', split_axis=0, concat_axis=0, tiled=True)  52.8 us
    all_to_all x1, waiting for transfers between devices, on_device(): lax.all_to_all(jnp.stack([shared_prompt_cache] * lax.axis_size(('req', 'e...  51.8 us
    gather x2, local copies, waits for them, and re-layouts, on_device(): jnp.take(returned.reshape(slot_total, -1), destination, axis=0)  16.3 us
    reduce_sum x1, other arithmetic, on_device(): jnp.sum(gates[..., None] * picked, axis=1)  16.2 us
    another operation x5, other arithmetic  12.5 us
    all_to_all x1, starting transfers between devices, on_device(): lax.all_to_all(jnp.stack([shared_prompt_cache] * lax.axis_size(('req', 'e...  10.7 us
    dot_general x1, matrix products, on_device(): jnp.einsum('sxcd,xdf->sxcf', arranged, expert_gate_up, preferred_element_...  9.72 us
  transfers between devices with their start and end apart: 2, of which 2 were waited for; matrix products, arithmetic and copies ran while one was open for 18% of the time, Pallas kernels for 0%

profile of v1, /device:TPU:32, one launch (start us, length us, event | category | flops | bytes accessed | tf_op | source)
XLA Modules:
  0.0 343.2 jit_solution(6650079622471130804)
XLA Ops:
  0.0 5.3 %stack.2 = bf16[128,4,16,512]{3,2,1,0:T(8,128)(2,1)} broadcast(bf16[4,16,512]{2,1,0:T(8,128)(2,1)} %param.24), dimensions={1,2,3} | broadcast | bytes 8454144 | tf_op jit(solution)/shard_map/stack | solution.py:203
  5.3 10.7 %all-to-all-start = ((bf16[128,4,16,512]{3,2,1,0:T(8,128)(2,1)}), bf16[128,4,16,512]{3,2,1,0:T(8,128)(2,1)}, u32[]{:S(2)}, u32[]{:S(2)}) async-start(bf16[128,4,16,512]{3,2,1,0:T(8,128)(2,1)} %stack.2), calls=%async_computation | async-start | bytes 16777216 | tf_op jit(solution)/shard_map/all_to_all | solution.py:202
  18.7 9.0 %reduce-window.6 = s32[32,8,128]{2,1,0:T(8,128)S(1)} reduce-window(s32[32,8,128]{2,1,0:T(8,128)S(1)} %fusion.53, s32[]{:T(128)} %constant.133.clone.1), window={size=1x1x128 pad=0_0x0_0x127_0}, to_apply=%region_10.11 | reduce-window | flops 4161536 | bytes 262148 | tf_op jit(solution)/shard_map/reduce-window
  33.4 2.8 fusion.75
  40.2 4.9 %fusion.73 = f32[256,1536]{1,0:T(8,128)} fusion(bf16[1536,1536]{1,0:T(8,128)(2,1)} %param.27, bf16[256,1536]{1,0:T(8,128)(2,1)S(1)} %copy-done.4, f32[1536]{0:T(1024)S(1)} %convert_element_type.85, f32[256]{0:T(256)S(1)} %add_rsqrt_fusion.1), kind=kOutput, calls=%fused_computation.157 | convolution fusion | flops 1209532416 | bytes 7085056 | tf_op jit(solution)/shard_map/dot_general | solution.py:72
  45.1 4.1 %convolution_add_fusion.1 = f32[256,1536]{1,0:T(8,128)} fusion(f32[256,1536]{1,0:T(8,128)} %fusion.73, bf16[256,1536]{1,0:T(8,128)(2,1)} %param.31, bf16[1536,256]{1,0:T(8,128)(2,1)} %param.30, s32[256]{0:T(256)S(1)} %and_select_fusion, s32[256]{0:T(256)S(1)} %get-tuple-element.5, bf16[256,1536]{1,0:T(8,128)(2,1)S(1)} %copy-done.4, ...), kind=kOutput, calls=%fused_computation.27 | convolution fusion | flops 404815872 | bytes 5514240 | tf_op jit(solution)/shard_map/dot_general | solution.py:44
  49.2 3.1 copy.78
  64.8 3.8 %fusion.14 = (f32[256,2,6]{0,2,1:T(8,128)S(1)}, f32[2,256,256,6]{2,1,3,0:T(8,128)}) fusion(pred[256,256]{0,1:T(8,128)(4,1)S(1)} %fusion.38, bf16[256,2,6,64]{3,0,2,1:T(8,128)(2,1)} %bitcast.122, bf16[256,2,6,64]{3,0,2,1:T(8,128)(2,1)S(1)} %bitcast.120, bf16[256,2,64]{2,0,1:T(8,128)(2,1)S(1)} %get-tuple-element.14, bf16[256,2,64]{2,0,1:T(8,128)(2,1)S(1)} %get-tuple-element.13), kind=kOutput, calls=%fused_computation.32 | convolution fusion | flops 205517824 | bytes 4141056 | tf_op jit(solution)/shard_map/tkgd,nkd->tkgn/dot_general | solution.py:127
  68.6 51.8 %all-to-all-done = bf16[128,4,16,512]{3,2,1,0:T(8,128)(2,1)} async-done(((bf16[128,4,16,512]{3,2,1,0:T(8,128)(2,1)}), bf16[128,4,16,512]{3,2,1,0:T(8,128)(2,1)}, u32[]{:S(2)}, u32[]{:S(2)}) %all-to-all-start) | async-done | bytes 8388640 | tf_op jit(solution)/shard_map/all_to_all | solution.py:202
  120.4 5.1 %gather_fusion.1 = bf16[64,16,512]{2,1,0:T(8,128)(2,1)} fusion(bf16[512,16,512]{2,1,0:T(8,128)(2,1)} %bitcast.10, s32[1024]{0:T(1024)S(1)} %pad_clamp_fusion.1), kind=kCustom, calls=%fused_computation.1 | custom fusion | bytes 2097408 | tf_op jit(solution)/shard_map/jit(_take)/gather | solution.py:207
  129.1 3.8 %fusion.2 = (f32[256,2,6]{0,2,1:T(8,128)S(1)}, f32[2,1024,256,6]{2,1,3,0:T(8,128)S(1)}) fusion(pred[256,1024]{0,1:T(8,128)(4,1)S(1)} %broadcast_compare_fusion, bf16[256,2,6,64]{3,0,2,1:T(8,128)(2,1)} %bitcast.123, bf16[256,2,6,64]{3,0,2,1:T(8,128)(2,1)S(1)} %bitcast.121, bf16[1024,4,128]{2,0,1:T(8,128)(2,1)S(1)} %copy_select_fusion), kind=kOutput, calls=%fused_computation.9 | convolution fusion | flops 816313344 | bytes 14561280 | tf_op jit(solution)/shard_map/tkgd,nkd->tkgn/dot_general | solution.py:127
  138.4 4.4 %fusion.25 = bf16[256,2,6,128]{0,3,2,1:T(8,128)(2,1)S(1)} fusion(f32[2,128,256,6]{2,1,3,0:T(8,128)} %fusion.22, f32[2,1024,256,6]{2,1,3,0:T(8,128)S(1)} %get-tuple-element.25, f32[256,2,6]{0,2,1:T(8,128)S(1)} %get-tuple-element.18, pred[256,1024]{0,1:T(8,128)(4,1)S(1)} %broadcast_compare_fusion, f32[256,2,6]{0,2,1:T(8,128)S(1)} %get-tuple-element.9, ...), kind=kOutput, calls=%fused_computation.44 | convolution fusion | flops 819855360 | bytes 15794176 | tf_op jit(solution)/shard_map/tkgn,nkd->tkgd/dot_general | solution.py:137
  143.7 5.0 %fusion.78 = f32[256,1536]{1,0:T(8,128)} fusion(bf16[256,1536]{0,1:T(8,128)(2,1)S(1)} %bitcast.125, bf16[1536,1536]{1,0:T(8,128)(2,1)} %param.29), kind=kOutput, calls=%fused_computation.160 | convolution fusion | flops 1207959552 | bytes 7077888 | tf_op jit(solution)/shard_map/dot_general | solution.py:97
  148.7 4.3 %multiply_reduce_fusion.1 = (f32[256]{0:T(256)S(1)}, f32[256,1536]{1,0:T(8,128)}) fusion(f32[256,1536]{1,0:T(8,128)} %fusion.78, bf16[256,1536]{1,0:T(8,128)(2,1)} %param.33, bf16[256,1536]{0,1:T(8,128)(2,1)} %bitcast.126, bf16[1536,256]{1,0:T(8,128)(2,1)} %param.32, s32[256]{0:T(256)S(1)} %copy-done.25, s32[256]{0:T(256)S(1)} %copy-done.20, ...), kind=kOutput, calls=%fused_computation.49 | convolution fusion | flops 405602048 | bytes 6294528 | tf_op jit(solution)/shard_map/dot_general | solution.py:44
  154.7 6.2 %gather_fusion.2 = bf16[1536,1536]{1,0:T(8,128)(2,1)} fusion(bf16[256,1536]{1,0:T(8,128)(2,1)S(1)} %multiply_convert_fusion, s32[2048]{0:T(1024)S(1)} %copy-done.14), kind=kCustom, calls=%fused_computation.2 | custom fusion | bytes 9443328 | tf_op jit(solution)/shard_map/jit(_take)/gather | solution.py:245
  163.7 61.6 %all_to_all.15 = bf16[32,48,1536]{2,1,0:T(8,128)(2,1)S(1)} all-to-all(bf16[32,48,1536]{2,1,0:T(8,128)(2,1)S(1)} %select_select_fusion), channel_id=1, replica_groups=mesh['req'=4,'exp'=32] {'exp'}, dimensions={0} | all-to-all | bytes 9437184 | tf_op jit(solution)/shard_map/all_to_all | solution.py:248
  225.3 9.7 %convolution_bitcast_fusion = f32[32,1,48,1536]{3,2,0,1:T(8,128)S(1)} fusion(bf16[32,48,1536]{2,1,0:T(8,128)(2,1)S(1)} %all_to_all.15, bf16[1,1536,1536]{2,1,0:T(8,128)(2,1)} %param.36), kind=kOutput, calls=%fused_computation.16 | convolution fusion | flops 7247757312 | bytes 18874368 | tf_op jit(solution)/shard_map/sxcd,xdf->sxcf/dot_general | solution.py:252
  235.0 5.5 %convolution_convert_fusion = bf16[32,48,1536]{2,1,0:T(8,128)(2,1)} fusion(f32[32,1,48,1536]{3,2,0,1:T(8,128)S(1)} %convolution_bitcast_fusion, bf16[1,768,1536]{2,1,0:T(8,128)(2,1)S(1)} %copy-done), kind=kOutput, calls=%fused_computation.22 | convolution fusion | flops 3629776896 | bytes 16515072 | tf_op jit(solution)/shard_map/sxcf,xfd->sxcd/dot_general | solution.py:257
  240.5 5.9 %all-to-all-start.2 = ((bf16[32,48,1536]{2,1,0:T(8,128)(2,1)}), bf16[32,48,1536]{2,1,0:T(8,128)(2,1)}, u32[]{:S(2)}, u32[]{:S(2)}) async-start(bf16[32,48,1536]{2,1,0:T(8,128)(2,1)} %convolution_convert_fusion), calls=%async_computation.2 | async-start | bytes 9437184 | tf_op jit(solution)/shard_map/all_to_all | solution.py:261
  247.7 8.7 %gather_fusion.4 = f32[1024]{0:T(1024)S(1)} fusion(f32[256,32]{0,1:T(8,128)S(1)} %fusion.79, s32[1024]{0:T(1024)S(1)} %reshape.472), kind=kCustom, calls=%fused_computation.4 | custom fusion | bytes 16384 | tf_op jit(solution)/shard_map/jit(take_along_axis)/gather | solution.py:108
  256.8 52.8 %all-to-all-done.2 = bf16[32,48,1536]{2,1,0:T(8,128)(2,1)} async-done(((bf16[32,48,1536]{2,1,0:T(8,128)(2,1)}), bf16[32,48,1536]{2,1,0:T(8,128)(2,1)}, u32[]{:S(2)}, u32[]{:S(2)}) %all-to-all-start.2) | async-done | bytes 4718624 | tf_op jit(solution)/shard_map/all_to_all | solution.py:261
  309.5 10.2 %gather_fusion.3 = bf16[1024,1536]{1,0:T(8,128)(2,1)} fusion(bf16[1536,1536]{1,0:T(8,128)(2,1)} %bitcast.32, s32[1024]{0:T(1024)S(1)} %broadcast_clamp_fusion), kind=kCustom, calls=%fused_computation.3 | custom fusion | bytes 6295552 | tf_op jit(solution)/shard_map/jit(_take)/gather | solution.py:262
  319.8 6.1 %gather.33 = bf16[256,4,1536]{2,1,0:T(4,128)(2,1)} reshape(bf16[1024,1536]{1,0:T(8,128)(2,1)} %gather_fusion.3) | data formatting | bytes 6291456 | tf_op jit(solution)/shard_map/jit(_take)/gather | solution.py:262
  325.9 16.2 %multiply_reduce_fusion = f32[256,1536]{1,0:T(8,128)S(1)} fusion(bf16[256,4,1536]{2,1,0:T(4,128)(2,1)} %gather.33, f32[256,4]{1,0:T(8,128)S(1)} %copy.88, pred[256,4]{1,0:T(8,128)(4,1)S(1)} %copy.94), kind=kLoop, calls=%fused_computation.10 | loop fusion | flops 5898240 | bytes 4723712 | tf_op jit(solution)/shard_map/reduce_sum | solution.py:264
  (142 shorter events, 41.7 us)
Async XLA Ops:
  0.0 235.0 %copy-start = (bf16[1,768,1536]{2,1,0:T(8,128)(2,1)S(1)}, bf16[1,768,1536]{2,1,0:T(8,128)(2,1)}, u32[]{:S(2)}) copy-start(bf16[1,768,1536]{2,1,0:T(8,128)(2,1)} %param.37) | copy-start | bytes 7077892
  5.3 10.8 %copy-start.26 = (s32[512]{0:T(512)S(1)}, s32[512]{0:T(512)}, u32[]{:S(2)}) copy-start(s32[512]{0:T(512)} %param.23) | copy-start | bytes 6148
  5.3 10.8 %copy-start.28 = (s32[4]{0:T(128)S(1)}, s32[4]{0:T(128)}, u32[]{:S(2)}) copy-start(s32[4]{0:T(128)} %param.21) | copy-start | bytes 52
  5.3 12.2 %copy-start.12 = (s32[256,4]{0,1:T(4,128)S(1)}, s32[256,4]{0,1:T(4,128)}, u32[]{:S(2)}) copy-start(s32[256,4]{0,1:T(4,128)} %param.25) | copy-start | bytes 12292
  5.3 12.6 %copy-start.22 = (bf16[1536]{0:T(1024)(128)(2,1)S(1)}, bf16[1536]{0:T(1024)(128)(2,1)}, u32[]{:S(2)}) copy-start(bf16[1536]{0:T(1024)(128)(2,1)} %param.26) | copy-start | bytes 9220
  5.3 12.6 %copy-start.23 = (bf16[1536]{0:T(1024)(128)(2,1)S(1)}, bf16[1536]{0:T(1024)(128)(2,1)}, u32[]{:S(2)}) copy-start(bf16[1536]{0:T(1024)(128)(2,1)} %param.34) | copy-start | bytes 9220
  5.3 25.8 %copy-start.18 = (s32[1,256]{1,0:T(1,128)S(1)}, s32[1,256]{1,0:T(1,128)}, u32[]{:S(2)}) copy-start(s32[1,256]{1,0:T(1,128)} %param.20) | copy-start | bytes 3076
  5.3 25.9 %copy-start.27 = (s32[4]{0:T(128)S(1)}, s32[4]{0:T(128)}, u32[]{:S(2)}) copy-start(s32[4]{0:T(128)} %param.22) | copy-start | bytes 52
  5.3 27.8 %copy-start.4 = (bf16[256,1536]{1,0:T(8,128)(2,1)S(1)}, bf16[256,1536]{1,0:T(8,128)(2,1)}, u32[]{:S(2)}) copy-start(bf16[256,1536]{1,0:T(8,128)(2,1)} %param.19) | copy-start | bytes 2359300
  5.3 115.1 %all-to-all-start = ((bf16[128,4,16,512]{3,2,1,0:T(8,128)(2,1)}), bf16[128,4,16,512]{3,2,1,0:T(8,128)(2,1)}, u32[]{:S(2)}, u32[]{:S(2)}) async-start(bf16[128,4,16,512]{3,2,1,0:T(8,128)(2,1)} %stack.2), calls=%async_computation | async-start | bytes 16777216 | tf_op jit(solution)/shard_map/all_to_all | solution.py:202
  30.4 9.7 %copy-start.15 = (s32[1536]{0:T(1024)}, s32[1536]{0:T(1024)S(1)}, u32[]{:S(2)}) copy-start(s32[1536]{0:T(1024)S(1)} %select_reduce_fusion) | copy-start | bytes 18436
  31.3 13.8 %copy-start.19 = (s32[256]{0:T(256)}, s32[256]{0:T(256)S(1)}, u32[]{:S(2)}) copy-start(s32[256]{0:T(256)S(1)} %get-tuple-element.5) | copy-start | bytes 3076
  31.7 13.4 %copy-start.7 = (f32[256,64]{0,1:T(8,128)}, f32[256,64]{0,1:T(8,128)S(1)}, u32[]{:S(2)}) copy-start(f32[256,64]{0,1:T(8,128)S(1)} %get-tuple-element.20) | copy-start | bytes 196612
  31.7 13.4 %copy-start.9 = (f32[256,64]{0,1:T(8,128)}, f32[256,64]{0,1:T(8,128)S(1)}, u32[]{:S(2)}) copy-start(f32[256,64]{0,1:T(8,128)S(1)} %get-tuple-element.21) | copy-start | bytes 196612
  68.6 59.0 %copy-start.21 = (pred[1024]{0:T(1024)(128)(4,1)S(1)}, pred[1024]{0:T(1024)(128)(4,1)}, u32[]{:S(2)}) copy-start(pred[1024]{0:T(1024)(128)(4,1)} %broadcast_in_dim.194) | copy-start | bytes 3076
  143.7 5.0 %copy-start.20 = (s32[256]{0:T(256)S(1)}, s32[256]{0:T(256)}, u32[]{:S(2)}) copy-start(s32[256]{0:T(256)} %copy-done.19) | copy-start | bytes 3076
  143.7 5.0 %copy-start.25 = (s32[256]{0:T(256)S(1)}, s32[256]{0:T(256)}, u32[]{:S(2)}) copy-start(s32[256]{0:T(256)} %copy-done.24) | copy-start | bytes 3076
  148.7 6.0 %copy-start.14 = (s32[2048]{0:T(1024)S(1)}, s32[2048]{0:T(1024)}, u32[]{:S(2)}) copy-start(s32[2048]{0:T(1024)} %pad_clamp_fusion) | copy-start | bytes 24580
  154.7 6.2 %copy-start.16 = (pred[32,48]{1,0:T(8,128)(4,1)S(1)}, pred[32,48]{1,0:T(8,128)(4,1)}, u32[]{:S(2)}) copy-start(pred[32,48]{1,0:T(8,128)(4,1)} %compare_and_fusion) | copy-start | bytes 4612
  154.7 6.2 %copy-start.17 = (pred[32,48]{1,0:T(8,128)(4,1)S(1)}, pred[32,48]{1,0:T(8,128)(4,1)}, u32[]{:S(2)}) copy-start(pred[32,48]{1,0:T(8,128)(4,1)} %broadcast_in_dim.200) | copy-start | bytes 4612
  240.5 6.9 %copy-start.13 = (bf16[1536,32]{0,1:T(8,128)(2,1)S(1)}, bf16[1536,32]{0,1:T(8,128)(2,1)}, u32[]{:S(2)}) copy-start(bf16[1536,32]{0,1:T(8,128)(2,1)} %param.35) | copy-start | bytes 294916
  240.5 69.1 %all-to-all-start.2 = ((bf16[32,48,1536]{2,1,0:T(8,128)(2,1)}), bf16[32,48,1536]{2,1,0:T(8,128)(2,1)}, u32[]{:S(2)}, u32[]{:S(2)}) async-start(bf16[32,48,1536]{2,1,0:T(8,128)(2,1)} %convolution_convert_fusion), calls=%async_computation.2 | async-start | bytes 9437184 | tf_op jit(solution)/shard_map/all_to_all | solution.py:261
  325.9 16.3 %copy-start.3 = (f32[256,1536]{1,0:T(8,128)S(1)}, f32[256,1536]{1,0:T(8,128)}, u32[]{:S(2)}) copy-start(f32[256,1536]{1,0:T(8,128)} %get-tuple-element.27) | copy-start | bytes 4718596
  325.9 17.3 %copy-start.1 = (bf16[1,768,1536]{2,1,0:T(8,128)(2,1)S(1)}, bf16[1,768,1536]{2,1,0:T(8,128)(2,1)}, u32[]{:S(2)}) copy-start(bf16[1,768,1536]{2,1,0:T(8,128)(2,1)} %param.37) | copy-start | bytes 7077892
  (7 other events, 21.7 us)
